TPU v7x, 32 devices: a whole 2x2x4 slice. The times are simulated.
32 devices in a mesh: groups: 2 (over x), ctx: 16 (over z, y, core).
Axes of the slice: x: 2, y: 2, z: 4, core: 2. Of those that a mesh axis runs over, the one named last changes fastest.
Arguments:
- queries: bfloat16 [4096, 1024], P(('groups', 'ctx')), parts along dimension 0, may hold values from -27 to 27
- keys: bfloat16 [4096, 1024], P(('groups', 'ctx')), parts along dimension 0, may hold values from -6 to 6
- values: bfloat16 [4096, 1024], P(('groups', 'ctx')), parts along dimension 0, may hold values from -6 to 6
- resid: bfloat16 [4096, 2048], P(('groups', 'ctx')), parts along dimension 0, may hold values from -6 to 6
- out_proj: bfloat16 [1024, 2048], replicated, may hold values from -0.1875 to 0.1875
- norm_gain: float32 [2048], replicated, may hold values from 0.25 to 1.75
- up_proj: bfloat16 [2048, 4096], P(None, 'ctx'), may hold values from -0.125 to 0.125
- down_proj: bfloat16 [2048, 4096], P(None, 'ctx'), may hold values from -0.09375 to 0.09375
- router: bfloat16 [2048, 2], replicated, may hold values from -0.125 to 0.125
- expert_ids: int32 [4096, 1], P(('groups', 'ctx')), parts along dimension 0, may hold values from 0 to 1; in each aligned block of 128 rows (0 to 127, 128 to 255, ...) at most 80 rows name the same one
- expert_in: bfloat16 [16, 2048, 512], P('ctx'), may hold values from -0.125 to 0.125
- expert_out: bfloat16 [16, 512, 2048], P('ctx'), may hold values from -0.09375 to 0.09375
Outputs:
- layer_out: bfloat16 [4096, 2048], P(('groups', 'ctx')), parts along dimension 0
There are 2 independent parts, one for each index of `groups`. A program takes and returns all parts, laid end to end along the dimension named above; an argument that names none is the same for every part. Nothing has to cross between parts.
Inputs may be any that keep to these rules, and one draw needn't show every extreme that they name: `expert_ids`: among the 128 tokens of one index of ctx, at most 80 name the same expert; in every draw some index of ctx has 80 tokens naming one expert.
All inputs are finite; a program needn't handle non-finite values.
Results may differ from a plain program's by a relative error of at most 0.0075.
Values may be sent and summed in bfloat16 or wider, within the bound.
No kernel may reach another device: no remote copies, remote signals or barrier semaphores. Data moves between devices by JAX's collectives and lax.ppermute only.
A program may use at most 192 MiB of HBM per device.

v0:
```python
import jax
import jax.numpy as jnp
from jax import lax
from jax.sharding import PartitionSpec as P

DH = 128
SPLIT = 8
NEG_FILL = -1e30
EPSILON = 1e-06


def from_partner(array, axis, apart):
    return lax.ppermute(array, axis, [(i, i ^ 1 << apart) for i in range(lax.axis_size(axis))])


def update_state(state, query_rows, query_offset, key_block, value_block, key_offset):
    maxima, totals, numer = state
    count_query = query_rows.shape[0]
    count_keys = key_block.shape[0]
    head_count = query_rows.shape[1] // DH
    query_heads = query_rows.reshape(count_query, head_count, DH)
    key_heads = key_block.reshape(count_keys, head_count, DH)
    value_heads = value_block.reshape(count_keys, head_count, DH)
    scores = jnp.einsum(
        "qhd,khd->hqk", query_heads, key_heads, preferred_element_type=jnp.float32
    ) * DH ** (-0.5)
    query_positions = query_offset + jnp.arange(count_query, dtype=jnp.int32)
    key_positions = key_offset + jnp.arange(count_keys, dtype=jnp.int32)
    visible = (key_positions[None, :] <= query_positions[:, None])[None]
    masked = jnp.where(visible, scores, NEG_FILL)
    new_max = jnp.maximum(maxima, jnp.max(masked, axis=2))
    weights = jnp.where(visible, jnp.exp(masked - new_max[..., None]), 0.0)
    factor = jnp.exp(maxima - new_max)
    totals = totals * factor + jnp.sum(weights, axis=2)
    numer = numer * factor[..., None] + jnp.einsum(
        "hqk,khd->hqd",
        weights.astype(jnp.bfloat16),
        value_heads,
        preferred_element_type=jnp.float32,
    )
    return (new_max, totals, numer)


def attend(query_sets, keys, values):
    head_count = keys.shape[1] // DH
    initial = []
    for query_rows, query_offset in query_sets:
        count_query = query_rows.shape[0]
        initial.append(
            (
                jnp.full((head_count, count_query), NEG_FILL, jnp.float32),
                jnp.zeros((head_count, count_query), jnp.float32),
                jnp.zeros((head_count, count_query, DH), jnp.float32),
            )
        )
    states = tuple(initial)
    key_offset = jnp.int32(0)
    key_whole = lax.all_gather(keys, "ctx", axis=0, tiled=True)
    value_whole = lax.all_gather(values, "ctx", axis=0, tiled=True)
    total_keys = key_whole.shape[0]
    step_rows = min(total_keys, 1024)
    for begin in range(0, total_keys, step_rows):
        key_block = key_whole[begin : begin + step_rows]
        value_block = value_whole[begin : begin + step_rows]
        block_offset = key_offset + begin
        query_rows, query_offset = query_sets[0]
        needed = block_offset <= query_offset + query_rows.shape[0] - 1
        updated = [
            lax.cond(
                needed,
                lambda carried, rows_now=query_rows, offset_now=query_offset, keys_now=key_block, values_now=value_block, start_now=block_offset: update_state(
                    carried, rows_now, offset_now, keys_now, values_now, start_now
                ),
                lambda carried: carried,
                states[0],
            )
        ]
        states = tuple(updated)
    results = []
    for maxima, totals, numer in states:
        result = (numer / totals[..., None]).astype(jnp.bfloat16)
        results.append(
            jnp.transpose(result, (1, 0, 2)).reshape(result.shape[1], result.shape[0] * DH)
        )
    return results


def body(
    queries,
    keys,
    values,
    resid,
    out_proj,
    norm_gain,
    up_proj,
    down_proj,
    router,
    expert_ids,
    expert_in,
    expert_out,
):
    tok_rows = queries.shape[0]
    width = resid.shape[1]
    live_count = router.shape[1]
    ctx_count = lax.axis_size("ctx")
    device_index = lax.axis_index("ctx")
    base_offset = device_index * tok_rows
    attn = attend([(queries, base_offset)], keys, values)[0]
    mixed = resid.astype(jnp.float32) + jnp.dot(attn, out_proj, preferred_element_type=jnp.float32)
    normed = (
        mixed * lax.rsqrt(jnp.mean(mixed * mixed, axis=1, keepdims=True) + EPSILON) * norm_gain
    ).astype(jnp.bfloat16)
    mlp_blocks = jnp.stack([up_proj, down_proj], 0)
    for level in range(live_count.bit_length() - 1):
        other_block = from_partner(mlp_blocks, "ctx", level)
        mlp_blocks = jnp.concatenate([mlp_blocks, other_block], axis=2)
    slots_per = max(2, 5 * tok_rows // (4 * live_count))
    chosen = expert_ids[:, 0]
    onehot = (chosen[:, None] == jnp.arange(live_count, dtype=jnp.int32)[None, :]).astype(
        jnp.bfloat16
    )
    row_iota = jnp.arange(tok_rows, dtype=jnp.int32)
    strictly_lower = (row_iota[None, :] < row_iota[:, None]).astype(jnp.bfloat16)
    counts_before = jnp.dot(strictly_lower, onehot, preferred_element_type=jnp.float32)
    slot_index = jnp.sum(onehot.astype(jnp.float32) * counts_before, axis=1).astype(jnp.int32)
    target_slot = chosen * slots_per + slot_index
    dispatch_matrix = (
        jnp.arange(live_count * slots_per, dtype=jnp.int32)[:, None] == target_slot[None, :]
    ).astype(jnp.bfloat16)
    packed = jnp.dot(dispatch_matrix, normed, preferred_element_type=jnp.float32).astype(
        jnp.bfloat16
    )
    sending = jnp.broadcast_to(
        packed.reshape(1, live_count, slots_per, width), (SPLIT, live_count, slots_per, width)
    )
    sending = sending.reshape(ctx_count, 1, slots_per, width)
    own_expert = device_index % live_count
    router_column = lax.dynamic_slice_in_dim(router, own_expert, 1, 1)
    weight_in = expert_in[0]
    weight_out = expert_out[0]
    received = lax.all_to_all(sending, "ctx", split_axis=0, concat_axis=1, tiled=True)
    rows = received.reshape(-1, width)
    expert_hidden = jax.nn.gelu(
        jnp.dot(rows, weight_in, preferred_element_type=jnp.float32)
    ).astype(jnp.bfloat16)
    mlp_hidden = jax.nn.gelu(
        jnp.dot(rows, mlp_blocks[0], preferred_element_type=jnp.float32)
    ).astype(jnp.bfloat16)
    gate = jax.nn.sigmoid(jnp.dot(rows, router_column, preferred_element_type=jnp.float32))
    produced = gate * jnp.dot(expert_hidden, weight_out, preferred_element_type=jnp.float32)
    produced = produced + lax.dot_general(
        mlp_hidden, mlp_blocks[1], (((1,), (1,)), ((), ())), preferred_element_type=jnp.float32
    )
    came_back = lax.all_to_all(
        produced.astype(jnp.bfloat16).reshape(received.shape),
        "ctx",
        split_axis=1,
        concat_axis=0,
        tiled=True,
    )
    summed = jnp.sum(
        came_back.astype(jnp.float32).reshape(SPLIT, live_count * slots_per, width), axis=0
    )
    mixture_part = lax.dot_general(
        dispatch_matrix.astype(jnp.float32),
        summed,
        (((0,), (0,)), ((), ())),
        precision=lax.Precision.HIGHEST,
        preferred_element_type=jnp.float32,
    )
    return (mixed + mixture_part).astype(jnp.bfloat16)


def solution(mesh):
    placed = (
        P(("groups", "ctx"), None),
        P(("groups", "ctx"), None),
        P(("groups", "ctx"), None),
        P(("groups", "ctx"), None),
        P(),
        P(),
        P(None, "ctx"),
        P(None, "ctx"),
        P(),
        P(("groups", "ctx"), None),
        P("ctx", None, None),
        P("ctx", None, None),
    )
    return jax.shard_map(
        body, mesh=mesh, in_specs=placed, out_specs=P(("groups", "ctx"), None), check_vma=False
    )
```

profile of v0, /device:TPU:1, one launch (start us, length us, event | category | flops | bytes accessed | tf_op | source)
XLA Modules:
  0.0 418.6 jit_solution(9774764442608556047)
XLA Ops:
  6.5 1.9 copy.30
  8.6 1.8 copy.31
  10.4 0.9 fusion.63
  12.0 52.5 %all-gather.3.cloned.1.call-done = bf16[2048,1024]{0,1:T(8,128)(2,1)} async-done(((bf16[128,1024]{0,1:T(8,128)(2,1)}), bf16[2048,1024]{0,1:T(8,128)(2,1)}) %all-gather.3.cloned.1.call-update) | async-done | bytes 4194320 | tf_op jit(solution)/shard_map/all_gather | solution.py:58
  64.5 52.8 %all-gather.5.cloned.1.call-done = bf16[2048,1024]{0,1:T(8,128)(2,1)} async-done(((bf16[128,1024]{0,1:T(8,128)(2,1)}), bf16[2048,1024]{0,1:T(8,128)(2,1)}) %all-gather.5.cloned.1.call-update) | async-done | bytes 4194320 | tf_op jit(solution)/shard_map/all_gather | solution.py:59
  117.3 9.7 %conditional.2 = (f32[8,128]{1,0:T(8,128)}, f32[8,128]{1,0:T(8,128)S(1)}, f32[8,128,128]{2,1,0:T(8,128)S(1)}) conditional(s32[]{:T(128)} %convert_element_type.67, () %tuple.20, (s32[]{:T(128)}, bf16[128,1024]{1,0:T(8,128)(2,1)}, bf16[2048,1024]{0,1:T(8,128)(2,1)}, bf16[2048,1024]{0,1:T(8,128)(2,1)}) %tuple.21), branch_computations={%region_0.0_spmd, %region_1.4_spmd} | conditional | flops 550768768 | bytes 44348500 | solution.py:69
  117.5 1.9 slice.24
  119.4 0.7 copy-done.2
  120.4 1.1 fusion
  122.1 2.2 fusion.10
  124.4 2.0 fusion.2
  127.3 3.1 multiply_reduce_fusion
  130.9 3.0 broadcast_in_dim.74
  133.8 13.3 %all-to-all-start = ((bf16[16,1,80,2048]{3,2,1,0:T(8,128)(2,1)}), bf16[16,1,80,2048]{3,2,1,0:T(8,128)(2,1)}, u32[]{:S(2)}, u32[]{:S(2)}) async-start(bf16[16,1,80,2048]{3,2,1,0:T(8,128)(2,1)} %bitcast.67), calls=%async_computation | async-start | bytes 10485760 | tf_op jit(solution)/shard_map/all_to_all | solution.py:141
  147.2 3.1 pad_maximum_fusion.1
  150.4 4.3 %collective-permute-done = bf16[2,2048,256]{2,1,0:T(8,128)(2,1)} collective-permute-done((bf16[2,2048,256]{2,1,0:T(8,128)(2,1)}, bf16[2,2048,256]{2,1,0:T(8,128)(2,1)}, u32[]{:S(2)}, u32[]{:S(2)}) %collective-permute-start) | collective-permute-done | bytes 2097184 | tf_op jit(solution)/shard_map/ppermute | solution.py:13
  154.8 3.6 pad_maximum_fusion
  158.4 85.2 %all-to-all-done = bf16[16,1,80,2048]{3,2,1,0:T(8,128)(2,1)} async-done(((bf16[16,1,80,2048]{3,2,1,0:T(8,128)(2,1)}), bf16[16,1,80,2048]{3,2,1,0:T(8,128)(2,1)}, u32[]{:S(2)}, u32[]{:S(2)}) %all-to-all-start) | async-done | bytes 5242912 | tf_op jit(solution)/shard_map/all_to_all | solution.py:141
  243.6 4.0 convolution_reduce_fusion
  247.6 11.0 %fusion.57 = f32[1280,2048]{1,0:T(8,128)} fusion(bf16[1,512,2048]{2,1,0:T(8,128)(2,1)S(1)} %copy-done, bf16[1280,2048]{1,0:T(8,128)(2,1)} %bitcast.9, bf16[1,2048,512]{2,1,0:T(8,128)(2,1)} %param.26), kind=kOutput, calls=%fused_computation.75 | convolution fusion | flops 5374607360 | bytes 19922944 | tf_op jit(solution)/shard_map/dot_general | solution.py:150
  258.5 12.2 %add_convert_fusion = bf16[1280,2048]{1,0:T(8,128)(2,1)} fusion(f32[1280,2048]{1,0:T(8,128)} %fusion.57, f32[1280]{0:T(1024)S(1)} %add_divide_fusion, bf16[2,2048,512]{2,1,0:T(8,128)(2,1)} %pad_maximum_fusion, bf16[1280,2048]{1,0:T(8,128)(2,1)} %bitcast.9), kind=kOutput, calls=%fused_computation.47 | convolution fusion | flops 5382471680 | bytes 25170944 | tf_op jit(solution)/shard_map/dot_general | solution.py:151
  270.8 138.5 %all_to_all.8 = bf16[1,16,80,2048]{3,2,0,1:T(8,128)(2,1)S(1)} all-to-all(bf16[1,16,80,2048]{3,2,0,1:T(8,128)(2,1)} %bitcast.71), channel_id=1, replica_groups=mesh['groups'=2,'ctx'=16] {'ctx'}, dimensions={1} | all-to-all | bytes 10485760 | tf_op jit(solution)/shard_map/all_to_all | solution.py:154
  409.2 1.0 convert_reduce_fusion
  410.2 1.6 fusion.55
  (28 shorter events, 3.5 us)
Async XLA Ops:
  6.5 241.0 %copy-start = (bf16[1,512,2048]{2,1,0:T(8,128)(2,1)S(1)}, bf16[1,512,2048]{2,1,0:T(8,128)(2,1)}, u32[]{:S(2)}) copy-start(bf16[1,512,2048]{2,1,0:T(8,128)(2,1)} %param.27) | copy-start | bytes 6291460
  6.5 57.9 %all-gather.3.cloned.1.call-start = ((), (), s32[]{:S(2)}) async-start(), calls=%async_computation.2 | async-start | bytes 4456448 | tf_op jit(solution)/shard_map/all_gather | solution.py:58
  8.5 108.8 %all-gather.5.cloned.1.call-start = ((), (), s32[]{:S(2)}) async-start(), calls=%async_computation.3 | async-start | bytes 4456448 | tf_op jit(solution)/shard_map/all_gather | solution.py:59
  117.3 2.8 copy-start.2
  117.5 2.9 copy-start.4
  127.2 3.2 copy-start.6
  133.8 109.8 %all-to-all-start = ((bf16[16,1,80,2048]{3,2,1,0:T(8,128)(2,1)}), bf16[16,1,80,2048]{3,2,1,0:T(8,128)(2,1)}, u32[]{:S(2)}, u32[]{:S(2)}) async-start(bf16[16,1,80,2048]{3,2,1,0:T(8,128)(2,1)} %bitcast.67), calls=%async_computation | async-start | bytes 10485760 | tf_op jit(solution)/shard_map/all_to_all | solution.py:141
  150.3 4.5 %collective-permute-start = (bf16[2,2048,256]{2,1,0:T(8,128)(2,1)}, bf16[2,2048,256]{2,1,0:T(8,128)(2,1)}, u32[]{:S(2)}, u32[]{:S(2)}) collective-permute-start(bf16[2,2048,256]{2,1,0:T(8,128)(2,1)} %pad_maximum_fusion.1), channel_id=1, source_target_pairs={{0,1},{1,0},{2,3},{3,2},{4,5},{5,4},{6,7},{7,6},{8,9},{9,8},{10,11... | collective-permute-start | bytes 6291464 | tf_op jit(solution)/shard_map/ppermute | solution.py:13
  150.4 93.1 %copy-start.7 = (bf16[2048,2]{0,1:T(2,128)(2,1)S(1)}, bf16[2048,2]{0,1:T(2,128)(2,1)}, u32[]{:S(2)}) copy-start(bf16[2048,2]{0,1:T(2,128)(2,1)} %param.24) | copy-start | bytes 24580
  409.2 2.5 copy-start.1
Sparse Core Ops, SparseCore 0:
  9.5 54.9 all-gather.2
  66.6 50.6 all-gather.4
where the time goes:
time: 419 us
  waiting for transfers between devices  195 us (47%)
  blocking collectives  138 us (33%)
  matrix products  36.5 us (9%)
  starting transfers between devices  13.5 us (3%)
  between operations  13.5 us (3%)
  other arithmetic  11.9 us (3%)
  local copies, waits for them, and re-layouts  9.79 us (2%)
    all_to_all x1, blocking collectives, body(): lax.all_to_all(produced.astype(jnp.bfloat16).reshape(received.shape), 'ct...  138 us
    all_to_all x1, waiting for transfers between devices, body(): lax.all_to_all(sending, 'ctx', split_axis=0, concat_axis=1, tiled=True)  85.2 us
    all_gather x1, waiting for transfers between devices, attend(): value_whole = lax.all_gather(values, 'ctx', axis=0, tiled=True)  52.8 us
    all_gather x1, waiting for transfers between devices, attend(): key_whole = lax.all_gather(keys, 'ctx', axis=0, tiled=True)  52.5 us
    all_to_all x1, starting transfers between devices, body(): lax.all_to_all(sending, 'ctx', split_axis=0, concat_axis=1, tiled=True)  13.3 us
    dot_general x1, matrix products, body(): lax.dot_general(mlp_hidden, mlp_blocks[1], (((1,), (1,)), ((), ())), pref...  12.2 us
    dot_general x1, matrix products, body(): jnp.dot(expert_hidden, weight_out, preferred_element_type=jnp.float32)  11 us
  transfers between devices with their start and end apart: 4, of which 4 were waited for; matrix products, arithmetic and copies ran while one was open for 2% of the time, Pallas kernels for 0%

commit v1 on v0

--- a/solution.py
+++ b/solution.py
@@ -56,7 +56,12 @@
     states = tuple(initial)
     key_offset = jnp.int32(0)
     key_whole = lax.all_gather(keys, "ctx", axis=0, tiled=True)
-    value_whole = lax.all_gather(values, "ctx", axis=0, tiled=True)
+    ring = [values]
+    for hop in range(15):
+        ring.append(lax.ppermute(ring[-1], "ctx", [(dev, (dev + 1) % 16) for dev in range(16)]))
+    value_whole = jnp.roll(
+        jnp.concatenate(ring[::-1], axis=0), (lax.axis_index("ctx") + 1) * ring[0].shape[0], axis=0
+    )
     total_keys = key_whole.shape[0]
     step_rows = min(total_keys, 1024)
     for begin in range(0, total_keys, step_rows):

time: 419 us -> 467 us (1.11)
  local copies, waits for them, and re-layouts: 9.79 us -> 29.6 us
  starting transfers between devices: 13.5 us -> 28.1 us
  waiting for transfers between devices: 195 us -> 207 us
    ppermute x0 -> x15, waiting for transfers between devices: none -> 118 us  [attend(): lax.ppermute(ring[-1], 'ctx', [(dev, (dev + 1) % 16) for dev in range(16)])]
    all_gather x1 -> x0, waiting for transfers between devices: 52.8 us -> none  [attend(): value_whole = lax.all_gather(values, 'ctx', axis=0, tiled=True)]
    all_gather x1, waiting for transfers between devices: 52.5 us -> 0.01 us  [attend(): key_whole = lax.all_gather(keys, 'ctx', axis=0, tiled=True)]
    unnamed x10 -> x77, local copies, waits for them, and re-layouts: 3.77 us -> 22 us
    ppermute x0 -> x15, starting transfers between devices: none -> 10.4 us  [attend(): lax.ppermute(ring[-1], 'ctx', [(dev, (dev + 1) % 16) for dev in range(16)])]
  transfers between devices with their start and end apart: 4 -> 18, of which waited for: 4 -> 17; matrix products, arithmetic and copies ran while one was open for 2% -> 5% of each run, Pallas kernels for 0% -> 0%
where the time goes in v1:
time: 467 us; the launch traced here: 466 us
  waiting for transfers between devices  207 us (44%)
  blocking collectives  138 us (30%)
  matrix products  36.5 us (8%)
  local copies, waits for them, and re-layouts  29.6 us (6%)
  starting transfers between devices  28.1 us (6%)
  between operations  13.9 us (3%)
  other arithmetic  12 us (3%)
    all_to_all x1, blocking collectives, body(): lax.all_to_all(produced.astype(jnp.bfloat16).reshape(received.shape), 'ct...  138 us
    ppermute x15, waiting for transfers between devices, attend(): lax.ppermute(ring[-1], 'ctx', [(dev, (dev + 1) % 16) for dev in range(16)])  118 us
    all_to_all x1, waiting for transfers between devices, body(): lax.all_to_all(sending, 'ctx', split_axis=0, concat_axis=1, tiled=True)  85 us
    unnamed x77, local copies, waits for them, and re-layouts  22 us
    all_to_all x1, starting transfers between devices, body(): lax.all_to_all(sending, 'ctx', split_axis=0, concat_axis=1, tiled=True)  17.5 us
    dot_general x1, matrix products, body(): lax.dot_general(mlp_hidden, mlp_blocks[1], (((1,), (1,)), ((), ())), pref...  12.2 us
    dot_general x1, matrix products, body(): jnp.dot(expert_hidden, weight_out, preferred_element_type=jnp.float32)  11 us
    ppermute x15, starting transfers between devices, attend(): lax.ppermute(ring[-1], 'ctx', [(dev, (dev + 1) % 16) for dev in range(16)])  10.4 us
  transfers between devices with their start and end apart: 18, of which 17 were waited for; matrix products, arithmetic and copies ran while one was open for 5% of the time, Pallas kernels for 0%

profile of v1, /device:TPU:1, one launch (start us, length us, event | category | flops | bytes accessed | tf_op | source)
XLA Modules:
  0.0 466.1 jit_solution(15907916775263489662)
XLA Ops:
  10.5 3.3 collective-permute-done
  22.1 4.9 %collective-permute-done.2 = bf16[128,1024]{0,1:T(8,128)(2,1)S(1)} collective-permute-done((bf16[128,1024]{0,1:T(8,128)(2,1)S(1)}, bf16[128,1024]{0,1:T(8,128)(2,1)S(1)}, u32[]{:S(2)}, u32[]{:S(2)}) %collective-permute-start.2) | collective-permute-done | bytes 262176 | tf_op jit(solution)/shard_map/ppermute | solution.py:61
  27.9 7.7 %collective-permute-done.3 = bf16[128,1024]{0,1:T(8,128)(2,1)S(1)} collective-permute-done((bf16[128,1024]{0,1:T(8,128)(2,1)S(1)}, bf16[128,1024]{0,1:T(8,128)(2,1)S(1)}, u32[]{:S(2)}, u32[]{:S(2)}) %collective-permute-start.3) | collective-permute-done | bytes 262176 | tf_op jit(solution)/shard_map/ppermute | solution.py:61
  36.5 12.8 %collective-permute-done.4 = bf16[128,1024]{0,1:T(8,128)(2,1)S(1)} collective-permute-done((bf16[128,1024]{0,1:T(8,128)(2,1)S(1)}, bf16[128,1024]{0,1:T(8,128)(2,1)S(1)}, u32[]{:S(2)}, u32[]{:S(2)}) %collective-permute-start.4) | collective-permute-done | bytes 262176 | tf_op jit(solution)/shard_map/ppermute | solution.py:61
  50.0 9.4 %collective-permute-done.5 = bf16[128,1024]{0,1:T(8,128)(2,1)S(1)} collective-permute-done((bf16[128,1024]{0,1:T(8,128)(2,1)S(1)}, bf16[128,1024]{0,1:T(8,128)(2,1)S(1)}, u32[]{:S(2)}, u32[]{:S(2)}) %collective-permute-start.5) | collective-permute-done | bytes 262176 | tf_op jit(solution)/shard_map/ppermute | solution.py:61
  61.0 11.6 %collective-permute-done.6 = bf16[128,1024]{0,1:T(8,128)(2,1)S(1)} collective-permute-done((bf16[128,1024]{0,1:T(8,128)(2,1)S(1)}, bf16[128,1024]{0,1:T(8,128)(2,1)S(1)}, u32[]{:S(2)}, u32[]{:S(2)}) %collective-permute-start.6) | collective-permute-done | bytes 262176 | tf_op jit(solution)/shard_map/ppermute | solution.py:61
  73.3 8.5 %collective-permute-done.7 = bf16[128,1024]{0,1:T(8,128)(2,1)S(1)} collective-permute-done((bf16[128,1024]{0,1:T(8,128)(2,1)S(1)}, bf16[128,1024]{0,1:T(8,128)(2,1)S(1)}, u32[]{:S(2)}, u32[]{:S(2)}) %collective-permute-start.7) | collective-permute-done | bytes 262176 | tf_op jit(solution)/shard_map/ppermute | solution.py:61
  82.6 8.5 %collective-permute-done.8 = bf16[128,1024]{0,1:T(8,128)(2,1)S(1)} collective-permute-done((bf16[128,1024]{0,1:T(8,128)(2,1)S(1)}, bf16[128,1024]{0,1:T(8,128)(2,1)S(1)}, u32[]{:S(2)}, u32[]{:S(2)}) %collective-permute-start.8) | collective-permute-done | bytes 262176 | tf_op jit(solution)/shard_map/ppermute | solution.py:61
  91.8 8.5 %collective-permute-done.9 = bf16[128,1024]{0,1:T(8,128)(2,1)S(1)} collective-permute-done((bf16[128,1024]{0,1:T(8,128)(2,1)S(1)}, bf16[128,1024]{0,1:T(8,128)(2,1)S(1)}, u32[]{:S(2)}, u32[]{:S(2)}) %collective-permute-start.9) | collective-permute-done | bytes 262176 | tf_op jit(solution)/shard_map/ppermute | solution.py:61
  101.0 8.5 %collective-permute-done.10 = bf16[128,1024]{0,1:T(8,128)(2,1)S(1)} collective-permute-done((bf16[128,1024]{0,1:T(8,128)(2,1)S(1)}, bf16[128,1024]{0,1:T(8,128)(2,1)S(1)}, u32[]{:S(2)}, u32[]{:S(2)}) %collective-permute-start.10) | collective-permute-done | bytes 262176 | tf_op jit(solution)/shard_map/ppermute | solution.py:61
  110.2 8.5 %collective-permute-done.11 = bf16[128,1024]{0,1:T(8,128)(2,1)S(1)} collective-permute-done((bf16[128,1024]{0,1:T(8,128)(2,1)S(1)}, bf16[128,1024]{0,1:T(8,128)(2,1)S(1)}, u32[]{:S(2)}, u32[]{:S(2)}) %collective-permute-start.11) | collective-permute-done | bytes 262176 | tf_op jit(solution)/shard_map/ppermute | solution.py:61
  119.4 8.5 %collective-permute-done.12 = bf16[128,1024]{0,1:T(8,128)(2,1)S(1)} collective-permute-done((bf16[128,1024]{0,1:T(8,128)(2,1)S(1)}, bf16[128,1024]{0,1:T(8,128)(2,1)S(1)}, u32[]{:S(2)}, u32[]{:S(2)}) %collective-permute-start.12) | collective-permute-done | bytes 262176 | tf_op jit(solution)/shard_map/ppermute | solution.py:61
  128.6 8.6 %collective-permute-done.13 = bf16[128,1024]{0,1:T(8,128)(2,1)} collective-permute-done((bf16[128,1024]{0,1:T(8,128)(2,1)S(1)}, bf16[128,1024]{0,1:T(8,128)(2,1)}, u32[]{:S(2)}, u32[]{:S(2)}) %collective-permute-start.13) | collective-permute-done | bytes 262176 | tf_op jit(solution)/shard_map/ppermute | solution.py:61
  138.9 7.2 %collective-permute-done.14 = bf16[128,1024]{0,1:T(8,128)(2,1)} collective-permute-done((bf16[128,1024]{0,1:T(8,128)(2,1)}, bf16[128,1024]{0,1:T(8,128)(2,1)}, u32[]{:S(2)}, u32[]{:S(2)}) %collective-permute-start.14) | collective-permute-done | bytes 262176 | tf_op jit(solution)/shard_map/ppermute | solution.py:61
  161.4 8.8 %conditional.2 = (f32[8,128]{1,0:T(8,128)}, f32[8,128]{1,0:T(8,128)S(1)}, f32[8,128,128]{2,1,0:T(8,128)S(1)}) conditional(s32[]{:T(128)} %convert_element_type.67, () %tuple.20, (s32[]{:T(128)}, bf16[128,1024]{1,0:T(8,128)(2,1)S(1)}, bf16[2048,1024]{0,1:T(8,128)(2,1)}, bf16[2048,1024]{0,1:T(8,128)(2,1)}) %tuple.37), branch_computations={%region_0.1_spmd, %region_1.4_spmd} | conditional | flops 550768768 | bytes 43299896 | solution.py:74
  170.6 3.1 multiply_reduce_fusion
  177.2 17.5 %all-to-all-start = ((bf16[16,1,80,2048]{3,2,1,0:T(8,128)(2,1)}), bf16[16,1,80,2048]{3,2,1,0:T(8,128)(2,1)}, u32[]{:S(2)}, u32[]{:S(2)}) async-start(bf16[16,1,80,2048]{3,2,1,0:T(8,128)(2,1)} %bitcast.67), calls=%async_computation | async-start | bytes 10485760 | tf_op jit(solution)/shard_map/all_to_all | solution.py:146
  198.0 4.3 collective-permute-done.15
  202.3 3.7 pad_maximum_fusion
  206.0 85.0 %all-to-all-done = bf16[16,1,80,2048]{3,2,1,0:T(8,128)(2,1)} async-done(((bf16[16,1,80,2048]{3,2,1,0:T(8,128)(2,1)}), bf16[16,1,80,2048]{3,2,1,0:T(8,128)(2,1)}, u32[]{:S(2)}, u32[]{:S(2)}) %all-to-all-start) | async-done | bytes 5242912 | tf_op jit(solution)/shard_map/all_to_all | solution.py:146
  291.1 4.0 convolution_reduce_fusion
  295.1 11.0 %fusion.57 = f32[1280,2048]{1,0:T(8,128)} fusion(bf16[1,512,2048]{2,1,0:T(8,128)(2,1)S(1)} %copy-done, bf16[1280,2048]{1,0:T(8,128)(2,1)} %bitcast.9, bf16[1,2048,512]{2,1,0:T(8,128)(2,1)} %param.26), kind=kOutput, calls=%fused_computation.75 | convolution fusion | flops 5374607360 | bytes 19922944 | tf_op jit(solution)/shard_map/dot_general | solution.py:155
  306.1 12.2 %add_convert_fusion = bf16[1280,2048]{1,0:T(8,128)(2,1)} fusion(f32[1280,2048]{1,0:T(8,128)} %fusion.57, f32[1280]{0:T(1024)S(1)} %add_divide_fusion, bf16[2,2048,512]{2,1,0:T(8,128)(2,1)} %pad_maximum_fusion, bf16[1280,2048]{1,0:T(8,128)(2,1)} %bitcast.9), kind=kOutput, calls=%fused_computation.47 | convolution fusion | flops 5382471680 | bytes 25170944 | tf_op jit(solution)/shard_map/dot_general | solution.py:156
  318.3 138.4 %all_to_all.8 = bf16[1,16,80,2048]{3,2,0,1:T(8,128)(2,1)S(1)} all-to-all(bf16[1,16,80,2048]{3,2,0,1:T(8,128)(2,1)} %bitcast.71), channel_id=1, replica_groups=mesh['groups'=2,'ctx'=16] {'ctx'}, dimensions={1} | all-to-all | bytes 10485760 | tf_op jit(solution)/shard_map/all_to_all | solution.py:159
  (122 shorter events, 56.6 us)
Async XLA Ops:
  6.5 288.5 %copy-start = (bf16[1,512,2048]{2,1,0:T(8,128)(2,1)S(1)}, bf16[1,512,2048]{2,1,0:T(8,128)(2,1)}, u32[]{:S(2)}) copy-start(bf16[1,512,2048]{2,1,0:T(8,128)(2,1)} %param.27) | copy-start | bytes 6291460
  6.5 154.8 %all-gather.2.cloned.1.call-start = ((), (), s32[]{:S(2)}) async-start(), calls=%async_computation.2 | async-start | bytes 4456448 | tf_op jit(solution)/shard_map/all_gather | solution.py:58
  7.8 6.0 %collective-permute-start = (bf16[128,1024]{0,1:T(8,128)(2,1)S(1)}, bf16[128,1024]{0,1:T(8,128)(2,1)S(1)}, u32[]{:S(2)}, u32[]{:S(2)}) collective-permute-start(bf16[128,1024]{0,1:T(8,128)(2,1)S(1)} %copy.33), channel_id=1, source_target_pairs={{0,1},{1,2},{2,3},{3,4},{4,5},{5,6},{6,7},{7,8},{8,9},{9,10},{10,1... | collective-permute-start | bytes 786440 | tf_op jit(solution)/shard_map/ppermute | solution.py:61
  13.8 5.8 %collective-permute-start.1 = (bf16[128,1024]{0,1:T(8,128)(2,1)S(1)}, bf16[128,1024]{0,1:T(8,128)(2,1)S(1)}, u32[]{:S(2)}, u32[]{:S(2)}) collective-permute-start(bf16[128,1024]{0,1:T(8,128)(2,1)S(1)} %collective-permute-done), channel_id=1, source_target_pairs={{0,1},{1,2},{2,3},{3,4},{4,5},{5,6},{6,7},{7,8},{8,9},{9,10},{10,1... | collective-permute-start | bytes 786440 | tf_op jit(solution)/shard_map/ppermute | solution.py:61
  19.6 7.3 %collective-permute-start.2 = (bf16[128,1024]{0,1:T(8,128)(2,1)S(1)}, bf16[128,1024]{0,1:T(8,128)(2,1)S(1)}, u32[]{:S(2)}, u32[]{:S(2)}) collective-permute-start(bf16[128,1024]{0,1:T(8,128)(2,1)S(1)} %collective-permute-done.1), channel_id=1, source_target_pairs={{0,1},{1,2},{2,3},{3,4},{4,5},{5,6},{6,7},{7,8},{8,9},{9,10},{10,1... | collective-permute-start | bytes 786440 | tf_op jit(solution)/shard_map/ppermute | solution.py:61
  26.9 8.7 %collective-permute-start.3 = (bf16[128,1024]{0,1:T(8,128)(2,1)S(1)}, bf16[128,1024]{0,1:T(8,128)(2,1)S(1)}, u32[]{:S(2)}, u32[]{:S(2)}) collective-permute-start(bf16[128,1024]{0,1:T(8,128)(2,1)S(1)} %collective-permute-done.2), channel_id=1, source_target_pairs={{0,1},{1,2},{2,3},{3,4},{4,5},{5,6},{6,7},{7,8},{8,9},{9,10},{10,1... | collective-permute-start | bytes 786440 | tf_op jit(solution)/shard_map/ppermute | solution.py:61
  35.6 13.7 %collective-permute-start.4 = (bf16[128,1024]{0,1:T(8,128)(2,1)S(1)}, bf16[128,1024]{0,1:T(8,128)(2,1)S(1)}, u32[]{:S(2)}, u32[]{:S(2)}) collective-permute-start(bf16[128,1024]{0,1:T(8,128)(2,1)S(1)} %collective-permute-done.3), channel_id=1, source_target_pairs={{0,1},{1,2},{2,3},{3,4},{4,5},{5,6},{6,7},{7,8},{8,9},{9,10},{10,1... | collective-permute-start | bytes 786440 | tf_op jit(solution)/shard_map/ppermute | solution.py:61
  50.0 9.4 %collective-permute-start.5 = (bf16[128,1024]{0,1:T(8,128)(2,1)S(1)}, bf16[128,1024]{0,1:T(8,128)(2,1)S(1)}, u32[]{:S(2)}, u32[]{:S(2)}) collective-permute-start(bf16[128,1024]{0,1:T(8,128)(2,1)S(1)} %collective-permute-done.4), channel_id=1, source_target_pairs={{0,1},{1,2},{2,3},{3,4},{4,5},{5,6},{6,7},{7,8},{8,9},{9,10},{10,1... | collective-permute-start | bytes 786440 | tf_op jit(solution)/shard_map/ppermute | solution.py:61
  60.1 12.5 %collective-permute-start.6 = (bf16[128,1024]{0,1:T(8,128)(2,1)S(1)}, bf16[128,1024]{0,1:T(8,128)(2,1)S(1)}, u32[]{:S(2)}, u32[]{:S(2)}) collective-permute-start(bf16[128,1024]{0,1:T(8,128)(2,1)S(1)} %collective-permute-done.5), channel_id=1, source_target_pairs={{0,1},{1,2},{2,3},{3,4},{4,5},{5,6},{6,7},{7,8},{8,9},{9,10},{10,1... | collective-permute-start | bytes 786440 | tf_op jit(solution)/shard_map/ppermute | solution.py:61
  73.3 8.5 %collective-permute-start.7 = (bf16[128,1024]{0,1:T(8,128)(2,1)S(1)}, bf16[128,1024]{0,1:T(8,128)(2,1)S(1)}, u32[]{:S(2)}, u32[]{:S(2)}) collective-permute-start(bf16[128,1024]{0,1:T(8,128)(2,1)S(1)} %collective-permute-done.6), channel_id=1, source_target_pairs={{0,1},{1,2},{2,3},{3,4},{4,5},{5,6},{6,7},{7,8},{8,9},{9,10},{10,1... | collective-permute-start | bytes 786440 | tf_op jit(solution)/shard_map/ppermute | solution.py:61
  82.5 8.5 %collective-permute-start.8 = (bf16[128,1024]{0,1:T(8,128)(2,1)S(1)}, bf16[128,1024]{0,1:T(8,128)(2,1)S(1)}, u32[]{:S(2)}, u32[]{:S(2)}) collective-permute-start(bf16[128,1024]{0,1:T(8,128)(2,1)S(1)} %collective-permute-done.7), channel_id=1, source_target_pairs={{0,1},{1,2},{2,3},{3,4},{4,5},{5,6},{6,7},{7,8},{8,9},{9,10},{10,1... | collective-permute-start | bytes 786440 | tf_op jit(solution)/shard_map/ppermute | solution.py:61
  91.8 8.5 %collective-permute-start.9 = (bf16[128,1024]{0,1:T(8,128)(2,1)S(1)}, bf16[128,1024]{0,1:T(8,128)(2,1)S(1)}, u32[]{:S(2)}, u32[]{:S(2)}) collective-permute-start(bf16[128,1024]{0,1:T(8,128)(2,1)S(1)} %collective-permute-done.8), channel_id=1, source_target_pairs={{0,1},{1,2},{2,3},{3,4},{4,5},{5,6},{6,7},{7,8},{8,9},{9,10},{10,1... | collective-permute-start | bytes 786440 | tf_op jit(solution)/shard_map/ppermute | solution.py:61
  101.0 8.5 %collective-permute-start.10 = (bf16[128,1024]{0,1:T(8,128)(2,1)S(1)}, bf16[128,1024]{0,1:T(8,128)(2,1)S(1)}, u32[]{:S(2)}, u32[]{:S(2)}) collective-permute-start(bf16[128,1024]{0,1:T(8,128)(2,1)S(1)} %collective-permute-done.9), channel_id=1, source_target_pairs={{0,1},{1,2},{2,3},{3,4},{4,5},{5,6},{6,7},{7,8},{8,9},{9,10},{10,1... | collective-permute-start | bytes 786440 | tf_op jit(solution)/shard_map/ppermute | solution.py:61
  110.2 8.5 %collective-permute-start.11 = (bf16[128,1024]{0,1:T(8,128)(2,1)S(1)}, bf16[128,1024]{0,1:T(8,128)(2,1)S(1)}, u32[]{:S(2)}, u32[]{:S(2)}) collective-permute-start(bf16[128,1024]{0,1:T(8,128)(2,1)S(1)} %collective-permute-done.10), channel_id=1, source_target_pairs={{0,1},{1,2},{2,3},{3,4},{4,5},{5,6},{6,7},{7,8},{8,9},{9,10},{10,1... | collective-permute-start | bytes 786440 | tf_op jit(solution)/shard_map/ppermute | solution.py:61
  119.4 8.5 %collective-permute-start.12 = (bf16[128,1024]{0,1:T(8,128)(2,1)S(1)}, bf16[128,1024]{0,1:T(8,128)(2,1)S(1)}, u32[]{:S(2)}, u32[]{:S(2)}) collective-permute-start(bf16[128,1024]{0,1:T(8,128)(2,1)S(1)} %collective-permute-done.11), channel_id=1, source_target_pairs={{0,1},{1,2},{2,3},{3,4},{4,5},{5,6},{6,7},{7,8},{8,9},{9,10},{10,1... | collective-permute-start | bytes 786440 | tf_op jit(solution)/shard_map/ppermute | solution.py:61
  128.6 8.6 %collective-permute-start.13 = (bf16[128,1024]{0,1:T(8,128)(2,1)S(1)}, bf16[128,1024]{0,1:T(8,128)(2,1)}, u32[]{:S(2)}, u32[]{:S(2)}) collective-permute-start(bf16[128,1024]{0,1:T(8,128)(2,1)S(1)} %collective-permute-done.12), channel_id=1, source_target_pairs={{0,1},{1,2},{2,3},{3,4},{4,5},{5,6},{6,7},{7,8},{8,9},{9,10},{10,1... | collective-permute-start | bytes 786440 | tf_op jit(solution)/shard_map/ppermute | solution.py:61
  137.2 8.8 %collective-permute-start.14 = (bf16[128,1024]{0,1:T(8,128)(2,1)}, bf16[128,1024]{0,1:T(8,128)(2,1)}, u32[]{:S(2)}, u32[]{:S(2)}) collective-permute-start(bf16[128,1024]{0,1:T(8,128)(2,1)} %collective-permute-done.13), channel_id=1, source_target_pairs={{0,1},{1,2},{2,3},{3,4},{4,5},{5,6},{6,7},{7,8},{8,9},{9,10},{10,1... | collective-permute-start | bytes 786440 | tf_op jit(solution)/shard_map/ppermute | solution.py:61
  138.1 16.7 %copy-start.9 = (bf16[128,1024]{0,1:T(8,128)(2,1)S(1)}, bf16[128,1024]{0,1:T(8,128)(2,1)}, u32[]{:S(2)}) copy-start(bf16[128,1024]{0,1:T(8,128)(2,1)} %copy-done.8) | copy-start | bytes 786436
  138.1 16.8 %copy-start.7 = (bf16[128,1024]{0,1:T(8,128)(2,1)S(1)}, bf16[128,1024]{0,1:T(8,128)(2,1)}, u32[]{:S(2)}) copy-start(bf16[128,1024]{0,1:T(8,128)(2,1)} %copy-done.6) | copy-start | bytes 786436
  138.1 16.9 %copy-start.5 = (bf16[128,1024]{0,1:T(8,128)(2,1)S(1)}, bf16[128,1024]{0,1:T(8,128)(2,1)}, u32[]{:S(2)}) copy-start(bf16[128,1024]{0,1:T(8,128)(2,1)} %copy-done.4) | copy-start | bytes 786436
  148.1 9.6 %copy-start.21 = (bf16[128,1024]{0,1:T(8,128)(2,1)S(1)}, bf16[128,1024]{0,1:T(8,128)(2,1)}, u32[]{:S(2)}) copy-start(bf16[128,1024]{0,1:T(8,128)(2,1)} %copy-done.20) | copy-start | bytes 786436
  177.2 113.9 %all-to-all-start = ((bf16[16,1,80,2048]{3,2,1,0:T(8,128)(2,1)}), bf16[16,1,80,2048]{3,2,1,0:T(8,128)(2,1)}, u32[]{:S(2)}, u32[]{:S(2)}) async-start(bf16[16,1,80,2048]{3,2,1,0:T(8,128)(2,1)} %bitcast.67), calls=%async_computation | async-start | bytes 10485760 | tf_op jit(solution)/shard_map/all_to_all | solution.py:146
  197.8 4.5 collective-permute-start.15
  198.0 93.1 %copy-start.23 = (bf16[2048,2]{0,1:T(2,128)(2,1)S(1)}, bf16[2048,2]{0,1:T(2,128)(2,1)}, u32[]{:S(2)}) copy-start(bf16[2048,2]{0,1:T(2,128)(2,1)} %param.24) | copy-start | bytes 24580
  (17 other events, 49.0 us)
Sparse Core Ops, SparseCore 0:
  18.2 58.4 all-gather.1
